TPU v7x, 256 devices: a whole 4x4x8 slice. The times are simulated.
256 devices in a mesh: section: 32 (over z_lo, x, core), tensor: 8 (over y, z_hi).
Axes of the slice: x: 4, y: 4, z: 8 (z_hi: 2, z_lo: 4; z = z_hi * 4 + z_lo), core: 2. Of those that a mesh axis runs over, the one named last changes fastest.
Arguments:
- forward_input: bfloat16 [32, 256, 8192], P('section', None, 'tensor'), may hold values from -6 to 6
- saved_last: bfloat16 [32, 256, 8192], P('section', None, 'tensor'), may hold values from -6 to 6
- saved_first: bfloat16 [32, 256, 8192], P('section', None, 'tensor'), may hold values from -6 to 6
- first_cotangent: bfloat16 [32, 256, 8192], P('section', None, 'tensor'), may hold values from -6 to 6
- section_entry: bfloat16 [256, 8192], P(None, 'tensor'), may hold values from -6 to 6
- last_gain: float32 [32, 8192], P('section'), may hold values from 0.1 to 1.9
- last_up: bfloat16 [32, 8192, 1024], P('section', None, 'tensor'), may hold values from -0.0625 to 0.0625
- last_down: bfloat16 [32, 1024, 8192], P('section', 'tensor'), may hold values from -0.1875 to 0.1875
- first_gain: float32 [32, 8192], P('section'), may hold values from 0.1 to 1.9
- first_up: bfloat16 [32, 8192, 1024], P('section', None, 'tensor'), may hold values from -0.0625 to 0.0625
- first_down: bfloat16 [32, 1024, 8192], P('section', 'tensor'), may hold values from -0.1875 to 0.1875
- head_gain: float32 [8192], replicated, may hold values from 0.1 to 1.9
- head_weight: float32 [8192, 4], P('tensor'), may hold values from -0.0625 to 0.0625
- head_bias: float32 [4], replicated, may hold values from -3 to 3
- prompt_length: int32 [1], replicated, may hold values from 8 to 248
- keep_mask: int32 [1, 256], replicated, may hold values 0 or 1
- target_box: int32 [1, 4], replicated, may hold values from 0 to 1000, as said below
Outputs:
- layer_output: bfloat16 [32, 256, 8192], P('section', None, 'tensor')
- input_gradient: bfloat16 [32, 256, 8192], P('section', None, 'tensor')
Inputs may be any that keep to these rules, and one draw needn't show every extreme that they name: `target_box`: each row is a box x1, y1, x2, y2 with x2 - x1 and y2 - y1 at least 100.
All inputs are finite; a program needn't handle non-finite values.
Results may differ from a plain program's by a relative error of at most 0.018.
Values may be sent and summed in bfloat16 or wider, within the bound.
A program may use at most 128 MiB of HBM per device.

v0:
```python
import jax
import jax.numpy as jnp
from jax import lax
from jax.sharding import PartitionSpec as P

epsilon = 1e-06
softness = 4.0
loss_scale = 4096.0


def shifted(value, axis, steps):
    count = lax.axis_size(axis)
    initial, last = (max(0, -steps), min(count, count - steps))
    return lax.ppermute(value, axis, [(source, source + steps) for source in range(initial, last)])


def unit_rows(values):
    values = values.astype(jnp.float32)
    inverse = lax.rsqrt(jnp.mean(values * values, axis=-1, keepdims=True) + epsilon)
    return (values * inverse, inverse)


def column_start(local_width):
    return lax.axis_index("tensor") * local_width


def column_slice(full_rows, local_width):
    return lax.dynamic_slice_in_dim(full_rows, column_start(local_width), local_width, 1)


def gather_columns(local_rows):
    return lax.all_gather(local_rows, "tensor", axis=1, tiled=True)


def reduce_columns(partial_rows):
    return lax.psum_scatter(
        partial_rows.astype(jnp.bfloat16), "tensor", scatter_dimension=1, tiled=True
    ).astype(jnp.float32)


def row_sums(values):
    return lax.psum(values, "tensor")


def layer_core(full_rows, gain_row, up_matrix, down_matrix):
    scaled, inverse = unit_rows(full_rows)
    normed = (scaled * gain_row).astype(jnp.bfloat16)
    activated = jax.nn.silu(jnp.dot(normed, up_matrix, preferred_element_type=jnp.float32)).astype(
        jnp.bfloat16
    )
    return jnp.dot(activated, down_matrix, preferred_element_type=jnp.float32)


def layer_backward(saved_rows, cotangent, gain_row, up_matrix, down_matrix):
    saved_full, cotangent_full = (
        lax.all_gather(saved_rows, "tensor", axis=1, tiled=True),
        lax.all_gather(cotangent, "tensor", axis=1, tiled=True),
    )
    scaled, inverse = unit_rows(saved_full)
    normed = (scaled * gain_row).astype(jnp.bfloat16)
    pre_act = jnp.dot(normed, up_matrix, preferred_element_type=jnp.float32)
    act_grad = lax.dot_general(
        cotangent_full, down_matrix, (((1,), (1,)), ((), ())), preferred_element_type=jnp.float32
    )
    sigmoid_pre = jax.nn.sigmoid(pre_act)
    pre_grad = (act_grad * sigmoid_pre * (1.0 + pre_act * (1.0 - sigmoid_pre))).astype(jnp.bfloat16)
    norm_partial = lax.dot_general(
        pre_grad, up_matrix, (((1,), (1,)), ((), ())), preferred_element_type=jnp.float32
    )
    norm_grad = reduce_columns(norm_partial)
    local_width = cotangent.shape[1]
    full_width = saved_full.shape[1]
    scaled_cols = column_slice(scaled, local_width)
    gain_cols = lax.dynamic_slice_in_dim(gain_row, column_start(local_width), local_width, 0)
    row_total = row_sums(jnp.sum(scaled_cols * gain_cols * norm_grad, axis=1))
    result = cotangent.astype(jnp.float32) + inverse * (
        gain_cols * norm_grad - scaled_cols * row_total[:, None] / full_width
    )
    return result.astype(jnp.bfloat16)


def soft_min(first, second):
    return 0.5 * (
        first + second - jnp.sqrt((first - second) * (first - second) + softness * softness)
    )


def soft_max(first, second):
    return 0.5 * (
        first + second + jnp.sqrt((first - second) * (first - second) + softness * softness)
    )


def soft_relu(difference):
    return 0.5 * (difference + jnp.sqrt(difference * difference + softness * softness))


def box_loss(logits, target_box):
    scaled_box = jax.nn.sigmoid(logits) * 1000.0
    centre_x = scaled_box[:, 0]
    centre_y = scaled_box[:, 1]
    box_width = scaled_box[:, 2]
    box_height = scaled_box[:, 3]
    left_pred = centre_x - 0.5 * box_width
    right_pred = centre_x + 0.5 * box_width
    lower_pred = centre_y - 0.5 * box_height
    upper_pred = centre_y + 0.5 * box_height
    target = target_box.astype(jnp.float32)
    inner_width = soft_relu(soft_min(right_pred, target[:, 2]) - soft_max(left_pred, target[:, 0]))
    inner_height = soft_relu(
        soft_min(upper_pred, target[:, 3]) - soft_max(lower_pred, target[:, 1])
    )
    intersection_area = inner_width * inner_height
    target_area = (target[:, 2] - target[:, 0]) * (target[:, 3] - target[:, 1])
    union_area = box_width * box_height + target_area - intersection_area
    outer_width = soft_max(right_pred, target[:, 2]) - soft_min(left_pred, target[:, 0])
    outer_height = soft_max(upper_pred, target[:, 3]) - soft_min(lower_pred, target[:, 1])
    enclosing = outer_width * outer_height
    return loss_scale * jnp.mean(
        1.0 - intersection_area / union_area + (enclosing - union_area) / enclosing
    )


def head_cotangent(
    final_rows, head_gain, head_weight, head_bias, prompt_length, keep_mask, target_box
):
    row_count = keep_mask.shape[0]
    positions = jnp.arange(keep_mask.shape[1], dtype=jnp.int32)[None, :]
    starts = prompt_length[:, None]
    weights = (positions == starts - 1).astype(jnp.float32) + (positions >= starts).astype(
        jnp.float32
    ) * keep_mask.astype(jnp.float32)
    counts = jnp.sum(weights, axis=1)
    local_width = final_rows.shape[1]
    full_width = local_width * lax.axis_size("tensor")
    tokens = final_rows.astype(jnp.float32).reshape(row_count, keep_mask.shape[1], local_width)
    pooled = (
        jnp.einsum("rt,rtd->rd", weights, tokens, precision=lax.Precision.HIGHEST) / counts[:, None]
    )
    gain_cols = lax.dynamic_slice_in_dim(head_gain, column_start(local_width), local_width, 0)
    logit_part = jnp.dot(pooled * gain_cols, head_weight, precision=lax.Precision.HIGHEST)
    square_part = jnp.sum(pooled * pooled, axis=1, keepdims=True)
    totals = row_sums(jnp.concatenate([logit_part, square_part], axis=1))
    inverse = lax.rsqrt(totals[:, 4] / full_width + epsilon)
    logits = totals[:, :4] * inverse[:, None] + head_bias

    def loss_of(logit_value):
        return box_loss(logit_value, target_box)

    loss_value, pullback = jax.vjp(loss_of, logits)
    logit_grad = pullback(jnp.ones((), jnp.float32))[0]
    scaled_grad = jnp.dot(logit_grad, head_weight.T, precision=lax.Precision.HIGHEST)
    unit_pooled = pooled * inverse[:, None]
    row_total = row_sums(jnp.sum(unit_pooled * gain_cols * scaled_grad, axis=1))
    pooled_grad = inverse[:, None] * (
        gain_cols * scaled_grad - unit_pooled * row_total[:, None] / full_width
    )
    token_grad = (weights / counts[:, None])[:, :, None] * pooled_grad[:, None, :]
    return token_grad.reshape(final_rows.shape[0], local_width).astype(jnp.bfloat16)


def per_device(
    forward_input,
    saved_last,
    saved_first,
    first_cotangent,
    section_entry,
    last_gain,
    last_up,
    last_down,
    first_gain,
    first_up,
    first_down,
    head_gain,
    head_weight,
    head_bias,
    prompt_length,
    keep_mask,
    target_box,
):
    section_index = lax.axis_index("section")
    opening = section_index == 0
    closing = section_index == lax.axis_size("section") - 1
    local_input = forward_input[0]
    gathered_input = gather_columns(local_input)
    last_partial = layer_core(gathered_input, last_gain[0], last_up[0], last_down[0])
    hidden_local = (local_input.astype(jnp.float32) + reduce_columns(last_partial)).astype(
        jnp.bfloat16
    )
    arrived_local = shifted(hidden_local, "section", 1)
    entry_local = jnp.where(opening, section_entry, arrived_local)
    entry_full = gather_columns(entry_local)
    first_partial = layer_core(entry_full, first_gain[0], first_up[0], first_down[0])
    layer_output = (entry_local.astype(jnp.float32) + reduce_columns(first_partial)).astype(
        jnp.bfloat16
    )
    first_grad = layer_backward(
        saved_first[0], first_cotangent[0], first_gain[0], first_up[0], first_down[0]
    )
    returned = shifted(first_grad, "section", -1)
    head_grad = head_cotangent(
        hidden_local, head_gain, head_weight, head_bias, prompt_length, keep_mask, target_box
    )
    cotangent = jnp.where(closing, head_grad, returned)
    saved_rows = jnp.where(closing, local_input, saved_last[0])
    input_gradient = layer_backward(saved_rows, cotangent, last_gain[0], last_up[0], last_down[0])
    return (layer_output[None], input_gradient[None])


def solution(mesh):
    placed = (
        P("section", None, "tensor"),
        P("section", None, "tensor"),
        P("section", None, "tensor"),
        P("section", None, "tensor"),
        P(None, "tensor"),
        P("section", None),
        P("section", None, "tensor"),
        P("section", "tensor", None),
        P("section", None),
        P("section", None, "tensor"),
        P("section", "tensor", None),
        P(),
        P("tensor", None),
        P(),
        P(),
        P(),
        P(),
    )
    return jax.shard_map(
        per_device,
        mesh=mesh,
        in_specs=placed,
        out_specs=(P("section", None, "tensor"), P("section", None, "tensor")),
        check_vma=False,
    )
```

profile of v0, /device:TPU:2, one launch (start us, length us, event | category | flops | bytes accessed | tf_op | source)
XLA Modules:
  0.0 1165.1 jit_solution(11418929649073457624)
XLA Ops:
  9.5 111.2 %all-gather.15.cloned.1.call-done = bf16[1,256,8192]{2,1,0:T(8,128)(2,1)} async-done(((bf16[1,256,1024]{2,1,0:T(8,128)(2,1)}), bf16[1,256,8192]{2,1,0:T(8,128)(2,1)}) %all-gather.15.cloned.1.call-update) | async-done | bytes 4194320 | tf_op jit(solution)/shard_map/all_gather | solution.py:32
  123.8 7.4 convolution_convert_fusion.3
  131.3 93.7 %all-gather.17.cloned.1.call-done = bf16[1,256,8192]{2,1,0:T(8,128)(2,1)} async-done(((bf16[1,256,1024]{2,1,0:T(8,128)(2,1)}), bf16[1,256,8192]{2,1,0:T(8,128)(2,1)}) %all-gather.17.cloned.1.call-update) | async-done | bytes 4194320 | tf_op jit(solution)/shard_map/all_gather | solution.py:56
  225.0 3.3 fusion.6
  231.5 97.9 %all-gather.19.cloned.1.call-done = bf16[1,256,8192]{2,1,0:T(8,128)(2,1)} async-done(((bf16[1,256,1024]{2,1,0:T(8,128)(2,1)}), bf16[1,256,8192]{2,1,0:T(8,128)(2,1)}) %all-gather.19.cloned.1.call-update) | async-done | bytes 4194320 | tf_op jit(solution)/shard_map/all_gather | solution.py:57
  329.4 9.9 convolution_convert_fusion.1
  346.2 108.6 %reduce-scatter.5.cloned.1.call-done = bf16[256,1024]{1,0:T(8,128)(2,1)} async-done(((bf16[256,8192]{1,0:T(8,128)(2,1)}), bf16[256,1024]{1,0:T(8,128)(2,1)}) %reduce-scatter.5.cloned.1.call-update) | async-done | bytes 524304 | tf_op jit(solution)/shard_map/reduce_scatter | solution.py:36
  459.1 6.6 convert_multiply_fusion.2
  465.7 25.8 %psum.28 = f32[1,5]{1,0:T(1,128)S(1)} all-reduce(f32[1,5]{1,0:T(1,128)S(1)} %pad_maximum_fusion), channel_id=1, replica_groups=mesh['section'=32,'tensor'=8] {'tensor'}, use_global_device_ids=true, to_apply=%region_6.7 | all-reduce | flops 5 | bytes 40 | tf_op jit(solution)/shard_map/psum | solution.py:42
  507.9 74.5 %reduce-scatter.9.cloned.1.call-done = bf16[256,1024]{1,0:T(8,128)(2,1)} async-done(((bf16[256,8192]{1,0:T(8,128)(2,1)}), bf16[256,1024]{1,0:T(8,128)(2,1)}) %reduce-scatter.9.cloned.1.call-update) | async-done | bytes 524304 | tf_op jit(solution)/shard_map/reduce_scatter | solution.py:36
  584.0 26.0 %all-reduce.4 = (f32[256]{0:T(256)S(1)}, f32[]{:T(128)}) all-reduce(f32[256]{0:T(256)S(1)} %fusion.68, f32[]{:T(128)} %multiply_reduce_fusion), channel_id=1, replica_groups=mesh['section'=32,'tensor'=8] {'tensor'}, use_global_device_ids=true, to_apply=%region_12.13 | all-reduce | flops 257 | bytes 2056 | tf_op jit(solution)/shard_map/psum | solution.py:42
  616.2 4.1 collective-permute-done.1
  622.2 3.7 collective-permute-start
  625.9 7.0 collective-permute-done
  633.8 54.6 %all-gather.21.cloned.1.call-done = bf16[1,256,8192]{2,1,0:T(8,128)(2,1)} async-done(((bf16[1,256,1024]{2,1,0:T(8,128)(2,1)}), bf16[1,256,8192]{2,1,0:T(8,128)(2,1)}) %all-gather.21.cloned.1.call-update) | async-done | bytes 4194320 | tf_op jit(solution)/shard_map/all_gather | solution.py:56
  688.4 3.3 fusion.7
  693.2 104.2 %all-gather.13.cloned.1.call-done = bf16[256,8192]{1,0:T(8,128)(2,1)} async-done(((bf16[256,1024]{1,0:T(8,128)(2,1)}), bf16[256,8192]{1,0:T(8,128)(2,1)}) %all-gather.13.cloned.1.call-update) | async-done | bytes 4194320 | tf_op jit(solution)/shard_map/all_gather | solution.py:57
  797.5 9.3 convolution_convert_fusion
  807.1 95.3 %all-gather.11.cloned.1.call-done = bf16[256,8192]{1,0:T(8,128)(2,1)} async-done(((bf16[256,1024]{1,0:T(8,128)(2,1)}), bf16[256,8192]{1,0:T(8,128)(2,1)}) %all-gather.11.cloned.1.call-update) | async-done | bytes 4194320 | tf_op jit(solution)/shard_map/all_gather | solution.py:32
  905.5 8.0 convolution_convert_fusion.2
  913.5 6.6 convert_multiply_fusion
  920.1 108.4 %reduce-scatter.11.cloned.1.call-done = bf16[256,1024]{1,0:T(8,128)(2,1)} async-done(((bf16[256,8192]{1,0:T(8,128)(2,1)}), bf16[256,1024]{1,0:T(8,128)(2,1)}) %reduce-scatter.11.cloned.1.call-update) | async-done | bytes 524304 | tf_op jit(solution)/shard_map/reduce_scatter | solution.py:36
  1030.1 25.3 %psum.31 = f32[256]{0:T(256)S(1)} all-reduce(f32[256]{0:T(256)S(1)} %fusion.73), channel_id=1, replica_groups=mesh['section'=32,'tensor'=8] {'tensor'}, use_global_device_ids=true, to_apply=%region_16.17 | all-reduce | flops 256 | bytes 2048 | tf_op jit(solution)/shard_map/psum | solution.py:42
  1058.0 98.2 %reduce-scatter.7.cloned.1.call-done = bf16[256,1024]{1,0:T(8,128)(2,1)} async-done(((bf16[256,8192]{1,0:T(8,128)(2,1)}), bf16[256,1024]{1,0:T(8,128)(2,1)}) %reduce-scatter.7.cloned.1.call-update) | async-done | bytes 524304 | tf_op jit(solution)/shard_map/reduce_scatter | solution.py:36
  (84 shorter events, 42.0 us)
Async XLA Ops:
  7.2 116.6 %copy-start = (bf16[1,8192,128]{2,1,0:T(8,128)(2,1)S(1)}, bf16[1,8192,128]{2,1,0:T(8,128)(2,1)}, u32[]{:S(2)}) copy-start(bf16[1,8192,128]{2,1,0:T(8,128)(2,1)} %param.23) | copy-start | bytes 6291460
  7.2 116.6 %copy-start.10 = (f32[1,8192]{1,0:T(1,128)S(1)}, f32[1,8192]{1,0:T(1,128)}, u32[]{:S(2)}) copy-start(f32[1,8192]{1,0:T(1,128)} %param.22) | copy-start | bytes 98308
  7.2 113.5 %all-gather.15.cloned.1.call-start = ((), (), s32[]{:S(2)}) async-start(), calls=%async_computation.10 | async-start | bytes 4718592 | tf_op jit(solution)/shard_map/all_gather | solution.py:32
  7.9 217.1 %all-gather.17.cloned.1.call-start = ((), (), s32[]{:S(2)}) async-start(), calls=%async_computation.11 | async-start | bytes 4718592 | tf_op jit(solution)/shard_map/all_gather | solution.py:56
  8.7 320.7 %all-gather.19.cloned.1.call-start = ((), (), s32[]{:S(2)}) async-start(), calls=%async_computation.12 | async-start | bytes 4718592 | tf_op jit(solution)/shard_map/all_gather | solution.py:57
  9.4 445.4 %reduce-scatter.5.cloned.1.call-start = ((), (), s32[]{:S(2)}) async-start(), calls=%async_computation.4 | async-start | bytes 4718592 | tf_op jit(solution)/shard_map/reduce_scatter | solution.py:36
  131.2 97.1 %copy-start.9 = (f32[1,8192]{1,0:T(1,128)S(1)}, f32[1,8192]{1,0:T(1,128)}, u32[]{:S(2)}) copy-start(f32[1,8192]{1,0:T(1,128)} %param.25) | copy-start | bytes 98308
  131.2 451.1 %reduce-scatter.9.cloned.1.call-start = ((), (), s32[]{:S(2)}) async-start(), calls=%async_computation.7 | async-start | bytes 4718592 | tf_op jit(solution)/shard_map/reduce_scatter | solution.py:36
  225.0 3.4 copy-start.2
  339.3 3.0 copy-start.14
  339.3 6.2 copy-start.12
  339.3 118.9 %copy-start.11 = (f32[1024,4]{0,1:T(4,128)S(1)}, f32[1024,4]{0,1:T(4,128)}, u32[]{:S(2)}) copy-start(f32[1024,4]{0,1:T(4,128)} %param.29) | copy-start | bytes 49156
  339.3 349.0 %all-gather.21.cloned.1.call-start = ((), (), s32[]{:S(2)}) async-start(), calls=%async_computation.13 | async-start | bytes 4718592 | tf_op jit(solution)/shard_map/all_gather | solution.py:56
  341.6 455.8 %all-gather.13.cloned.1.call-start = ((), (), s32[]{:S(2)}) async-start(), calls=%async_computation.8 | async-start | bytes 4718592 | tf_op jit(solution)/shard_map/all_gather | solution.py:57
  459.1 33.7 %copy-start.13 = (f32[4]{0:T(128)S(1)}, f32[4]{0:T(128)}, u32[]{:S(2)}) copy-start(f32[4]{0:T(128)} %param.30) | copy-start | bytes 52
  459.1 150.8 %copy-start.5 = (bf16[1,256,1024]{2,1,0:T(8,128)(2,1)S(1)}, bf16[1,256,1024]{2,1,0:T(8,128)(2,1)}, u32[]{:S(2)}) copy-start(bf16[1,256,1024]{2,1,0:T(8,128)(2,1)} %param.20) | copy-start | bytes 1572868
  611.7 8.6 collective-permute-start.1
  622.2 280.2 %all-gather.11.cloned.1.call-start = ((), (), s32[]{:S(2)}) async-start(), calls=%async_computation.5 | async-start | bytes 4718592 | tf_op jit(solution)/shard_map/all_gather | solution.py:32
  622.2 10.7 collective-permute-start
  633.8 394.7 %reduce-scatter.11.cloned.1.call-start = ((), (), s32[]{:S(2)}) async-start(), calls=%async_computation.9 | async-start | bytes 4718592 | tf_op jit(solution)/shard_map/reduce_scatter | solution.py:36
  688.4 3.4 copy-start.1
  806.8 349.4 %reduce-scatter.7.cloned.1.call-start = ((), (), s32[]{:S(2)}) async-start(), calls=%async_computation.6 | async-start | bytes 4718592 | tf_op jit(solution)/shard_map/reduce_scatter | solution.py:36
  913.5 141.9 %copy-start.7 = (bf16[256,1024]{1,0:T(8,128)(2,1)S(1)}, bf16[256,1024]{1,0:T(8,128)(2,1)}, u32[]{:S(2)}) copy-start(bf16[256,1024]{1,0:T(8,128)(2,1)} %copy-done.6) | copy-start | bytes 1572868
  920.1 236.2 %copy-start.4 = (bf16[256,1024]{1,0:T(8,128)(2,1)S(1)}, bf16[256,1024]{1,0:T(8,128)(2,1)}, u32[]{:S(2)}) copy-start(bf16[256,1024]{1,0:T(8,128)(2,1)} %broadcast_select_fusion.1) | copy-start | bytes 1572868
  (3 other events, 3.5 us)
Sparse Core Ops, SparseCore 0:
  10.7 109.9 all-gather.14
  123.3 101.6 all-gather.16
  227.7 101.6 all-gather.18
  333.4 121.3 reduce-scatter.4
  458.8 123.5 reduce-scatter.8
  585.4 102.8 all-gather.20
  691.0 106.4 all-gather.12
  800.7 101.6 all-gather.10
  906.6 121.8 reduce-scatter.10
  1032.5 123.7 reduce-scatter.6
where the time goes:
time: 1170 us
  waiting for transfers between devices  960 us (82%)
  blocking collectives  77.2 us (7%)
  other arithmetic  47.2 us (4%)
  matrix products  39.8 us (3%)
  between operations  30.4 us (3%)
    reduce_scatter x4, waiting for transfers between devices, reduce_columns(): lax.psum_scatter(partial_rows.astype(jnp.bfloat16), 'tensor', scatter_dim...  390 us
    all_gather x2, waiting for transfers between devices, gather_columns(): return lax.all_gather(local_rows, 'tensor', axis=1, tiled=True)  206 us
    all_gather x2, waiting for transfers between devices, layer_backward(): lax.all_gather(cotangent, 'tensor', axis=1, tiled=True)  202 us
    all_gather x2, waiting for transfers between devices, layer_backward(): lax.all_gather(saved_rows, 'tensor', axis=1, tiled=True)  148 us
    psum x3, blocking collectives, row_sums(): return lax.psum(values, 'tensor')  77.2 us
  transfers between devices with their start and end apart: 12, of which 12 were waited for; matrix products, arithmetic and copies ran while one was open for 7% of the time, Pallas kernels for 0%

commit v1 on v0

--- a/solution.py
+++ b/solution.py
@@ -29,7 +29,15 @@
 
 
 def gather_columns(local_rows):
-    return lax.all_gather(local_rows, "tensor", axis=1, tiled=True)
+    return jnp.concatenate(
+        lax.all_to_all(
+            jnp.stack([local_rows] * lax.axis_size("tensor"), axis=0),
+            axis_name="tensor",
+            split_axis=0,
+            concat_axis=0,
+        ),
+        axis=1,
+    )
 
 
 def reduce_columns(partial_rows):

time: 1170 us -> 1100 us (0.940)
  waiting for transfers between devices: 960 us -> 863 us
  starting transfers between devices: 6.2 us -> 20.3 us
    all_gather x2 -> x0, waiting for transfers between devices: 206 us -> none  [gather_columns(): return lax.all_gather(local_rows, 'tensor', axis=1, tiled=True)]
    all_to_all x0 -> x2, waiting for transfers between devices: none -> 78.2 us  [gather_columns(): lax.all_to_all(jnp.stack([local_rows] * lax.axis_size('tensor'), axis=0),...]
    all_gather x2, waiting for transfers between devices: 202 us -> 255 us  [layer_backward(): lax.all_gather(cotangent, 'tensor', axis=1, tiled=True)]
    all_to_all x0 -> x2, starting transfers between devices: none -> 15.8 us  [gather_columns(): lax.all_to_all(jnp.stack([local_rows] * lax.axis_size('tensor'), axis=0),...]
    all_gather x2, waiting for transfers between devices: 148 us -> 135 us  [layer_backward(): lax.all_gather(saved_rows, 'tensor', axis=1, tiled=True)]
  transfers between devices with their start and end apart: 12 -> 12, of which waited for: 12 -> 11; matrix products, arithmetic and copies ran while one was open for 7% -> 9% of each run, Pallas kernels for 0% -> 0%
where the time goes in v1:
time: 1100 us
  waiting for transfers between devices  863 us (78%)
  blocking collectives  77.1 us (7%)
  other arithmetic  56.7 us (5%)
  matrix products  39.9 us (4%)
  between operations  29.9 us (3%)
  starting transfers between devices  20.3 us (2%)
    reduce_scatter x4, waiting for transfers between devices, reduce_columns(): lax.psum_scatter(partial_rows.astype(jnp.bfloat16), 'tensor', scatter_dim...  383 us
    all_gather x2, waiting for transfers between devices, layer_backward(): lax.all_gather(cotangent, 'tensor', axis=1, tiled=True)  255 us
    all_gather x2, waiting for transfers between devices, layer_backward(): lax.all_gather(saved_rows, 'tensor', axis=1, tiled=True)  135 us
    all_to_all x2, waiting for transfers between devices, gather_columns(): lax.all_to_all(jnp.stack([local_rows] * lax.axis_size('tensor'), axis=0),...  78.2 us
    psum x3, blocking collectives, row_sums(): return lax.psum(values, 'tensor')  77.1 us
  transfers between devices with their start and end apart: 12, of which 11 were waited for; matrix products, arithmetic and copies ran while one was open for 9% of the time, Pallas kernels for 0%

profile of v1, /device:TPU:2, one launch (start us, length us, event | category | flops | bytes accessed | tf_op | source)
XLA Modules:
  0.0 1098.1 jit_solution(3362236316368695256)
XLA Ops:
  11.4 11.2 %all-to-all-start = ((bf16[8,256,1024]{1,2,0:T(8,128)(2,1)}), bf16[8,256,1024]{1,2,0:T(8,128)(2,1)}, u32[]{:S(2)}, u32[]{:S(2)}) async-start(bf16[8,256,1024]{1,2,0:T(8,128)(2,1)} %stack.4), calls=%async_computation | async-start | bytes 8388608 | tf_op jit(solution)/shard_map/all_to_all | solution.py:33
  24.8 78.2 %all-to-all-done = bf16[8,256,1024]{1,2,0:T(8,128)(2,1)} async-done(((bf16[8,256,1024]{1,2,0:T(8,128)(2,1)}), bf16[8,256,1024]{1,2,0:T(8,128)(2,1)}, u32[]{:S(2)}, u32[]{:S(2)}) %all-to-all-start) | async-done | bytes 4194336 | tf_op jit(solution)/shard_map/all_to_all | solution.py:33
  106.3 4.2 fusion.2
  110.5 7.3 convolution_convert_fusion.3
  117.8 68.3 %all-gather.11.cloned.1.call-done = bf16[1,256,8192]{2,1,0:T(8,128)(2,1)} async-done(((bf16[1,256,1024]{2,1,0:T(8,128)(2,1)}), bf16[1,256,8192]{2,1,0:T(8,128)(2,1)}) %all-gather.11.cloned.1.call-update) | async-done | bytes 4194320 | tf_op jit(solution)/shard_map/all_gather | solution.py:64
  192.6 101.0 %all-gather.13.cloned.1.call-done = bf16[1,256,8192]{2,1,0:T(8,128)(2,1)} async-done(((bf16[1,256,1024]{2,1,0:T(8,128)(2,1)}), bf16[1,256,8192]{2,1,0:T(8,128)(2,1)}) %all-gather.13.cloned.1.call-update) | async-done | bytes 4194320 | tf_op jit(solution)/shard_map/all_gather | solution.py:65
  293.6 9.9 convolution_convert_fusion.1
  310.6 109.1 %reduce-scatter.5.cloned.1.call-done = bf16[256,1024]{1,0:T(8,128)(2,1)} async-done(((bf16[256,8192]{1,0:T(8,128)(2,1)}), bf16[256,1024]{1,0:T(8,128)(2,1)}) %reduce-scatter.5.cloned.1.call-update) | async-done | bytes 524304 | tf_op jit(solution)/shard_map/reduce_scatter | solution.py:44
  424.1 6.6 convert_multiply_fusion
  430.6 25.7 %psum.28 = f32[1,5]{1,0:T(1,128)S(1)} all-reduce(f32[1,5]{1,0:T(1,128)S(1)} %pad_maximum_fusion), channel_id=1, replica_groups=mesh['section'=32,'tensor'=8] {'tensor'}, use_global_device_ids=true, to_apply=%region_6.7 | all-reduce | flops 5 | bytes 40 | tf_op jit(solution)/shard_map/psum | solution.py:50
  472.2 74.5 %reduce-scatter.9.cloned.1.call-done = bf16[256,1024]{1,0:T(8,128)(2,1)} async-done(((bf16[256,8192]{1,0:T(8,128)(2,1)}), bf16[256,1024]{1,0:T(8,128)(2,1)}) %reduce-scatter.9.cloned.1.call-update) | async-done | bytes 524304 | tf_op jit(solution)/shard_map/reduce_scatter | solution.py:44
  548.3 26.0 %all-reduce.4 = (f32[256]{0:T(256)S(1)}, f32[]{:T(128)}) all-reduce(f32[256]{0:T(256)S(1)} %fusion.61, f32[]{:T(128)} %multiply_reduce_fusion), channel_id=1, replica_groups=mesh['section'=32,'tensor'=8] {'tensor'}, use_global_device_ids=true, to_apply=%region_12.13 | all-reduce | flops 257 | bytes 2056 | tf_op jit(solution)/shard_map/psum | solution.py:50
  580.6 4.1 collective-permute-done.1
  586.5 66.2 %all-gather.7.cloned.1.call-done = bf16[256,8192]{1,0:T(8,128)(2,1)} async-done(((bf16[256,1024]{1,0:T(8,128)(2,1)}), bf16[256,8192]{1,0:T(8,128)(2,1)}) %all-gather.7.cloned.1.call-update) | async-done | bytes 4194320 | tf_op jit(solution)/shard_map/all_gather | solution.py:64
  659.3 7.1 collective-permute-done
  669.0 4.5 all-to-all-start.1
  673.6 153.6 %all-gather.9.cloned.1.call-done = bf16[256,8192]{1,0:T(8,128)(2,1)} async-done(((bf16[256,1024]{1,0:T(8,128)(2,1)}), bf16[256,8192]{1,0:T(8,128)(2,1)}) %all-gather.9.cloned.1.call-update) | async-done | bytes 4194320 | tf_op jit(solution)/shard_map/all_gather | solution.py:65
  827.2 9.4 convolution_convert_fusion
  840.9 4.2 fusion.5
  845.1 8.2 convolution_convert_fusion.2
  853.4 6.6 convert_multiply_fusion.2
  860.0 101.4 %reduce-scatter.11.cloned.1.call-done = bf16[256,1024]{1,0:T(8,128)(2,1)} async-done(((bf16[256,8192]{1,0:T(8,128)(2,1)}), bf16[256,1024]{1,0:T(8,128)(2,1)}) %reduce-scatter.11.cloned.1.call-update) | async-done | bytes 524304 | tf_op jit(solution)/shard_map/reduce_scatter | solution.py:44
  963.0 25.4 %psum.31 = f32[256]{0:T(256)S(1)} all-reduce(f32[256]{0:T(256)S(1)} %fusion.66), channel_id=1, replica_groups=mesh['section'=32,'tensor'=8] {'tensor'}, use_global_device_ids=true, to_apply=%region_16.17 | all-reduce | flops 256 | bytes 2048 | tf_op jit(solution)/shard_map/psum | solution.py:50
  991.0 98.2 %reduce-scatter.7.cloned.1.call-done = bf16[256,1024]{1,0:T(8,128)(2,1)} async-done(((bf16[256,8192]{1,0:T(8,128)(2,1)}), bf16[256,1024]{1,0:T(8,128)(2,1)}) %reduce-scatter.7.cloned.1.call-update) | async-done | bytes 524304 | tf_op jit(solution)/shard_map/reduce_scatter | solution.py:44
  (93 shorter events, 57.2 us)
Async XLA Ops:
  7.2 103.3 %copy-start = (bf16[1,8192,128]{2,1,0:T(8,128)(2,1)S(1)}, bf16[1,8192,128]{2,1,0:T(8,128)(2,1)}, u32[]{:S(2)}) copy-start(bf16[1,8192,128]{2,1,0:T(8,128)(2,1)} %param.23) | copy-start | bytes 6291460
  7.2 179.0 %all-gather.11.cloned.1.call-start = ((), (), s32[]{:S(2)}) async-start(), calls=%async_computation.12 | async-start | bytes 4718592 | tf_op jit(solution)/shard_map/all_gather | solution.py:64
  11.4 12.6 %copy-start.10 = (f32[1,8192]{1,0:T(1,128)S(1)}, f32[1,8192]{1,0:T(1,128)}, u32[]{:S(2)}) copy-start(f32[1,8192]{1,0:T(1,128)} %param.22) | copy-start | bytes 98308
  11.4 91.6 %all-to-all-start = ((bf16[8,256,1024]{1,2,0:T(8,128)(2,1)}), bf16[8,256,1024]{1,2,0:T(8,128)(2,1)}, u32[]{:S(2)}, u32[]{:S(2)}) async-start(bf16[8,256,1024]{1,2,0:T(8,128)(2,1)} %stack.4), calls=%async_computation | async-start | bytes 8388608 | tf_op jit(solution)/shard_map/all_to_all | solution.py:33
  22.6 271.0 %all-gather.13.cloned.1.call-start = ((), (), s32[]{:S(2)}) async-start(), calls=%async_computation.13 | async-start | bytes 4718592 | tf_op jit(solution)/shard_map/all_gather | solution.py:65
  23.4 396.3 %reduce-scatter.5.cloned.1.call-start = ((), (), s32[]{:S(2)}) async-start(), calls=%async_computation.6 | async-start | bytes 4718592 | tf_op jit(solution)/shard_map/reduce_scatter | solution.py:44
  117.8 71.7 %copy-start.9 = (f32[1,8192]{1,0:T(1,128)S(1)}, f32[1,8192]{1,0:T(1,128)}, u32[]{:S(2)}) copy-start(f32[1,8192]{1,0:T(1,128)} %param.25) | copy-start | bytes 98308
  117.8 428.9 %reduce-scatter.9.cloned.1.call-start = ((), (), s32[]{:S(2)}) async-start(), calls=%async_computation.8 | async-start | bytes 4718592 | tf_op jit(solution)/shard_map/reduce_scatter | solution.py:44
  186.2 3.4 copy-start.2
  303.6 3.2 copy-start.14
  303.6 6.4 copy-start.12
  303.6 119.6 %copy-start.11 = (f32[1024,4]{0,1:T(4,128)S(1)}, f32[1024,4]{0,1:T(4,128)}, u32[]{:S(2)}) copy-start(f32[1024,4]{0,1:T(4,128)} %param.29) | copy-start | bytes 49156
  303.6 349.1 %all-gather.7.cloned.1.call-start = ((), (), s32[]{:S(2)}) async-start(), calls=%async_computation.9 | async-start | bytes 4718592 | tf_op jit(solution)/shard_map/all_gather | solution.py:64
  305.9 521.3 %all-gather.9.cloned.1.call-start = ((), (), s32[]{:S(2)}) async-start(), calls=%async_computation.10 | async-start | bytes 4718592 | tf_op jit(solution)/shard_map/all_gather | solution.py:65
  424.1 33.6 %copy-start.13 = (f32[4]{0:T(128)S(1)}, f32[4]{0:T(128)}, u32[]{:S(2)}) copy-start(f32[4]{0:T(128)} %param.30) | copy-start | bytes 52
  424.1 150.3 %copy-start.4 = (bf16[1,256,1024]{2,1,0:T(8,128)(2,1)S(1)}, bf16[1,256,1024]{2,1,0:T(8,128)(2,1)}, u32[]{:S(2)}) copy-start(bf16[1,256,1024]{2,1,0:T(8,128)(2,1)} %param.20) | copy-start | bytes 1572868
  576.1 8.6 collective-permute-start.1
  652.7 5.2 copy-start.1
  656.0 10.5 collective-permute-start
  657.9 8.6 copy-start.8
  669.0 168.6 %all-to-all-start.1 = ((bf16[8,256,1024]{1,2,0:T(8,128)(2,1)}), bf16[8,256,1024]{1,2,0:T(8,128)(2,1)}, u32[]{:S(2)}, u32[]{:S(2)}) async-start(bf16[8,256,1024]{1,2,0:T(8,128)(2,1)} %stack.5), calls=%async_computation.2 | async-start | bytes 8388608 | tf_op jit(solution)/shard_map/all_to_all | solution.py:33
  673.5 287.9 %reduce-scatter.11.cloned.1.call-start = ((), (), s32[]{:S(2)}) async-start(), calls=%async_computation.11 | async-start | bytes 4718592 | tf_op jit(solution)/shard_map/reduce_scatter | solution.py:44
  836.6 252.6 %reduce-scatter.7.cloned.1.call-start = ((), (), s32[]{:S(2)}) async-start(), calls=%async_computation.7 | async-start | bytes 4718592 | tf_op jit(solution)/shard_map/reduce_scatter | solution.py:44
  853.4 135.0 %copy-start.6 = (bf16[256,1024]{1,0:T(8,128)(2,1)S(1)}, bf16[256,1024]{1,0:T(8,128)(2,1)}, u32[]{:S(2)}) copy-start(bf16[256,1024]{1,0:T(8,128)(2,1)} %copy-done.5) | copy-start | bytes 1572868
  (3 other events, 3.4 us)
Sparse Core Ops, SparseCore 0:
  10.7 175.4 all-gather.10
  188.8 104.7 all-gather.12
  297.8 121.8 reduce-scatter.4
  423.7 122.9 reduce-scatter.8
  549.8 102.8 all-gather.6
  655.8 171.3 all-gather.8
  836.7 124.6 reduce-scatter.10
  965.6 123.6 reduce-scatter.6
